TPU v7x, 128 devices: a whole 4x4x4 slice. The times are simulated.
128 devices in a mesh: gx: 64 (over y, x, z_hi, core), gy: 2 (over z_lo).
Axes of the slice: x: 4, y: 4, z: 4 (z_hi: 2, z_lo: 2; z = z_hi * 2 + z_lo), core: 2. Of those that a mesh axis runs over, the one named last changes fastest.
Arguments:
- adjoint_in: float32 [3, 1024, 128, 256], P(None, 'gx', 'gy'), may hold values from -6 to 6
- checkpoints: bfloat16 [2, 16384, 3, 2048], P(None, ('gx', 'gy')), may hold values from -4 to 4
- send_owner: int32 [16384], P(('gx', 'gy')), may hold values from 0 to 127, as said below
- receive_rows: int32 [16384], P(('gx', 'gy')), may hold values from 0 to 255, as said below
- block_columns: int32 [4096, 8], P(('gx', 'gy')), may hold values from 0 to 35
- eddy_blocks: bfloat16 [8, 128, 128], replicated, may hold values from -0.1875 to 0.1875
- thrust: float32 [80], replicated, may hold values from 0.4 to 1
- yaw_angle: float32 [80], replicated, may hold values from -0.5 to 0.5
- turbine_place: float32 [3, 80], replicated, may hold values from 0 to 1
- turbine_tile: int32 [80], replicated, may hold values from 0 to 127
- fringe_rows: int32 [128], replicated, may hold values from 0 to 1023, as said below
Outputs:
- adjoint_out: float32 [3, 1024, 128, 256], P(None, 'gx', 'gy')
- control_gradient: float32 [2, 80], replicated
Inputs may be any that keep to these rules, and one draw needn't show every extreme that they name: `send_owner`: each storage tile holds 128 slots; at most 2 of its slots name one owner, exactly 2 for some owners; every owner is named by 128 slots in all. `receive_rows`: for each owner the 128 entries name each row storage*2+rank of a slot sent to it exactly once. `fringe_rows`: distinct rows.
All inputs are finite; a program needn't handle non-finite values.
Results may differ from a plain program's by a relative error of at most 0.00086.
Values may be sent and summed in bfloat16 or wider, within the bound.
A program may use at most 128 MiB of HBM per device.

v0:
```python
import jax
import jax.numpy as jnp
from jax import lax
from jax.sharding import PartitionSpec as P

PB = 128
KB = 8
CAP = 2
NZB = 2
TIME_STEP = 0.25
BASE_VISC = 0.1
EDDY_COEF = 0.5
KERNEL_WIDTH = 1.5
FRINGE_KEEP = 0.5


def padded(block, sides, width):
    for axis, dim in sides:
        count = lax.axis_size(axis)
        forward = [(i, i + 1) for i in range(count - 1)]
        forward.append((count - 1, 0))
        backward = [(target, source) for source, target in forward]
        low = lax.ppermute(
            lax.slice_in_dim(block, block.shape[dim] - width, None, axis=dim), axis, forward
        )
        high = lax.ppermute(lax.slice_in_dim(block, 0, width, axis=dim), axis, backward)
        block = jnp.concatenate([low, block, high], axis=dim)
    return block


def turbine_terms(
    tile_index, thrust, yaw_angle, turbine_place, turbine_tile, width_x, width_y, height
):
    owned_mask = (turbine_tile == tile_index).astype(jnp.float32)
    spread = 2.0 * KERNEL_WIDTH * KERNEL_WIDTH
    along_x = jnp.exp(
        -(
            (jnp.arange(width_x, dtype=jnp.float32)[None, :] - turbine_place[0][:, None] * width_x)
            ** 2
        )
        / spread
    )
    along_y = jnp.exp(
        -(
            (jnp.arange(width_y, dtype=jnp.float32)[None, :] - turbine_place[1][:, None] * width_y)
            ** 2
        )
        / spread
    )
    along_z = jnp.exp(
        -(
            (
                jnp.arange(height, dtype=jnp.float32)[None, :]
                - turbine_place[2][:, None] * (0.5 * height)
            )
            ** 2
        )
        / spread
    )
    plan_kernel = (along_x[:, :, None] * along_y[:, None, :]).reshape(
        along_x.shape[0], width_x * width_y
    )
    cosine = jnp.cos(yaw_angle)
    loading = owned_mask * thrust * cosine * cosine
    drag_field = jnp.dot(
        (plan_kernel * loading[:, None]).T, along_z, precision=lax.Precision.HIGHEST
    )
    return (owned_mask, plan_kernel, along_z, drag_field.reshape(width_x, width_y, height))


def block_selector(columns, width_x):
    count_in = (width_x + 2) * NZB
    picks = (columns[:, :, None] == jnp.arange(count_in, dtype=jnp.int32)[None, None, :]).astype(
        jnp.bfloat16
    )
    return picks.reshape(width_x, NZB, KB, width_x + 2, NZB)


def advance(
    extended,
    forward,
    selector,
    eddy_blocks,
    owned_mask,
    plan_kernel,
    along_z,
    drag_field,
    fringe_scale,
):
    center = extended[:, 1:-1, 1:-1, :]
    east_cells = extended[:, 2:, 1:-1, :]
    west_cells = extended[:, :-2, 1:-1, :]
    north_cells = extended[:, 1:-1, 2:, :]
    south_cells = extended[:, 1:-1, :-2, :]
    zero_plane = jnp.zeros_like(center[..., :1])
    upper_cells = jnp.concatenate([center[..., 1:], zero_plane], axis=3)
    lower_cells = jnp.concatenate([zero_plane, center[..., :-1]], axis=3)
    velocity = forward.astype(jnp.float32)
    laplace = (
        east_cells
        + west_cells
        + north_cells
        + south_cells
        + upper_cells
        + lower_cells
        - 6.0 * center
    )
    advect = 0.5 * (
        velocity[0] * (east_cells - west_cells)
        + velocity[1] * (north_cells - south_cells)
        + velocity[2] * (upper_cells - lower_cells)
    )
    viscous = EDDY_COEF * jnp.sqrt(1.0 + jnp.sum(velocity * velocity, axis=0))
    components, width_x, width_y, height = center.shape
    planes = extended[:, :, 1:-1, :].astype(jnp.bfloat16)
    planes = planes.reshape(components, width_x + 2, width_y, NZB, PB)
    picked = jnp.einsum(
        "xbkqc,aqycz->xbkayz", selector, planes, preferred_element_type=jnp.float32
    ).astype(jnp.bfloat16)
    product = jnp.einsum(
        "xbkayz,kzw->axybw", picked, eddy_blocks, preferred_element_type=jnp.float32
    )
    product = product.reshape(components, width_x, width_y, height)
    update = center + TIME_STEP * (advect + BASE_VISC * laplace + viscous * product)
    drag_term = TIME_STEP * drag_field * velocity[0] * center[0]
    first_only = (jnp.arange(components, dtype=jnp.int32) == 0).astype(jnp.float32)
    update = update - first_only[:, None, None, None] * drag_term[None]
    update = update * fringe_scale[None, :, None, None]
    density = (velocity[0] * velocity[0] * center[0]).reshape(width_x * width_y, height)
    projected = jnp.dot(density, along_z.T, precision=lax.Precision.HIGHEST)
    gradient_part = owned_mask * jnp.sum(plan_kernel.T * projected, axis=0)
    return (update, gradient_part)


def shards(
    adjoint_in,
    checkpoints,
    send_owner,
    receive_rows,
    block_columns,
    eddy_blocks,
    thrust,
    yaw_angle,
    turbine_place,
    turbine_tile,
    fringe_rows,
):
    count_x = lax.axis_size("gx")
    count_y = lax.axis_size("gy")
    tile_count = count_x * count_y
    tile_index = lax.axis_index("gx") * count_y + lax.axis_index("gy")
    components, width_x, width_y, height = adjoint_in.shape
    steps_total = checkpoints.shape[0]
    block_shape = checkpoints.shape[2:]
    owner_ids = jnp.arange(tile_count, dtype=jnp.int32)
    onehot = (send_owner[:, None] == owner_ids[None, :]).astype(jnp.int32)
    slot_rank = jnp.sum(jnp.cumsum(onehot, axis=0) * onehot, axis=1) - 1
    position = send_owner * CAP + slot_rank
    row_ids = jnp.arange(tile_count * CAP, dtype=jnp.int32)
    pack_table = (row_ids[:, None] == position[None, :]).astype(jnp.bfloat16)
    pick_table = (receive_rows[:, None] == row_ids[None, :]).astype(jnp.bfloat16)
    selector = block_selector(block_columns, width_x)
    rows_x = lax.axis_index("gx") * width_x + jnp.arange(width_x, dtype=jnp.int32)
    fringe_hit = jnp.any(rows_x[:, None] == fringe_rows[None, :], axis=1)
    fringe_scale = jnp.where(fringe_hit, FRINGE_KEEP, 1.0).astype(jnp.float32)
    owned_mask, plan_kernel, along_z, drag_field = turbine_terms(
        tile_index, thrust, yaw_angle, turbine_place, turbine_tile, width_x, width_y, height
    )
    adjoint = adjoint_in
    gradient_sum = jnp.zeros((thrust.shape[0],), jnp.float32)
    for step_index in range(steps_total):
        stored = checkpoints[steps_total - 1 - step_index]
        packed = jnp.einsum(
            "rs,scb->rcb", pack_table, stored, preferred_element_type=jnp.float32
        ).astype(jnp.bfloat16)
        arrived = lax.all_to_all(
            packed.reshape((tile_count, CAP) + block_shape),
            ("gx", "gy"),
            split_axis=0,
            concat_axis=0,
            tiled=True,
        )
        arrived = arrived.reshape((tile_count * CAP,) + block_shape)
        forward = jnp.einsum(
            "jr,rcb->cjb", pick_table, arrived, preferred_element_type=jnp.float32
        ).astype(jnp.bfloat16)
        forward = forward.reshape(components, width_x, width_y, height)
        extended = padded(adjoint, (("gx", 1), ("gy", 2)), 1)
        adjoint, gradient_part = advance(
            extended,
            forward,
            selector,
            eddy_blocks,
            owned_mask,
            plan_kernel,
            along_z,
            drag_field,
            fringe_scale,
        )
        gradient_sum = gradient_sum + lax.psum(gradient_part, ("gx", "gy"))
    cosine = jnp.cos(yaw_angle)
    sine = jnp.sin(yaw_angle)
    control_gradient = jnp.stack(
        [
            -0.5 * TIME_STEP * cosine * cosine * gradient_sum,
            TIME_STEP * thrust * sine * cosine * gradient_sum,
        ]
    )
    return (adjoint, control_gradient)


def solution(mesh):
    return jax.shard_map(
        shards,
        mesh=mesh,
        in_specs=(
            P(None, "gx", "gy", None),
            P(None, ("gx", "gy"), None, None),
            P(("gx", "gy")),
            P(("gx", "gy")),
            P(("gx", "gy"), None),
            P(),
            P(),
            P(),
            P(),
            P(),
            P(),
        ),
        out_specs=(P(None, "gx", "gy", None), P()),
        check_vma=False,
    )
```

profile of v0, /device:TPU:1, one launch (start us, length us, event | category | flops | bytes accessed | tf_op | source)
XLA Modules:
  0.0 342.7 jit_solution(4182224922127656898)
XLA Ops:
  3.1 4.0 %convolution_convert_fusion.1 = bf16[256,3,2048]{2,0,1:T(8,128)(2,1)} fusion(bf16[2,128,3,2048]{3,1,2,0:T(8,128)(2,1)} %param.12, s32[128]{0:T(128)S(1)} %add_add_fusion), kind=kOutput, calls=%fused_computation.11 | convolution fusion | flops 404258816 | bytes 4719104 | tf_op jit(solution)/shard_map/rs,scb->rcb/dot_general | solution.py:173
  7.1 4.6 %reshape.194 = bf16[128,2,3,2048]{3,1,0,2:T(2,128)(2,1)S(1)} reshape(bf16[256,3,2048]{2,0,1:T(8,128)(2,1)} %convolution_convert_fusion.1) | data formatting | bytes 6291456 | tf_op jit(solution)/shard_map/reshape | solution.py:177
  11.7 3.8 %copy.121 = bf16[128,2,3,2048]{3,1,2,0:T(2,128)(2,1)} copy(bf16[128,2,3,2048]{3,1,0,2:T(2,128)(2,1)S(1)} %reshape.194) | data formatting | bytes 6291456 | tf_op jit(solution)/shard_map/reshape | solution.py:177
  15.6 11.9 %all-to-all-start = ((bf16[128,2,3,2048]{3,1,2,0:T(2,128)(2,1)}), bf16[128,2,3,2048]{3,1,2,0:T(2,128)(2,1)}, u32[]{:S(2)}, u32[]{:S(2)}) async-start(bf16[128,2,3,2048]{3,1,2,0:T(2,128)(2,1)} %copy.121), calls=%async_computation | async-start | bytes 6291456 | tf_op jit(solution)/shard_map/all_to_all | solution.py:176
  28.3 3.5 %collective-permute-start.1 = (f32[3,1,64,256]{3,2,1,0:T(8,128)}, f32[3,1,64,256]{3,2,1,0:T(8,128)}, u32[]{:S(2)}, u32[]{:S(2)}) collective-permute-start(f32[3,1,64,256]{3,2,1,0:T(8,128)} %get-tuple-element.24), channel_id=1, source_target_pairs={{0,2},{2,4},{4,6},{6,8},{8,10},{10,12},{12,14},{14,16},{16,18},{18... | collective-permute-start | bytes 589832 | tf_op jit(solution)/shard_map/ppermute | solution.py:23
  32.0 3.8 %fusion.65 = (f32[3,16,64,255]{3,2,1,0:T(8,128)}, f32[3,16,64,255]{3,2,1,0:T(8,128)}) fusion(f32[3,16,64,256]{3,2,1,0:T(8,128)S(1)} %copy-done.1), kind=kLoop, calls=%fused_computation.124 | loop fusion | bytes 12533760 | tf_op jit(solution)/shard_map/slice | solution.py:96
  35.8 2.6 convolution_convert_fusion
  39.7 2.0 mul.377
  41.8 1.8 multiply_bitcast_fusion.2
  43.6 2.0 copy.160
  45.7 6.0 %reshape.197 = bf16[128,2,3,2048]{3,1,0,2:T(2,128)(2,1)} reshape(bf16[256,3,2048]{2,0,1:T(8,128)(2,1)} %convolution_convert_fusion) | data formatting | bytes 6291456 | tf_op jit(solution)/shard_map/reshape | solution.py:177
  51.7 5.7 %copy.136 = bf16[128,2,3,2048]{3,1,2,0:T(2,128)(2,1)} copy(bf16[128,2,3,2048]{3,1,0,2:T(2,128)(2,1)} %reshape.197) | data formatting | bytes 6291456 | tf_op jit(solution)/shard_map/reshape | solution.py:177
  57.6 8.9 %collective-permute-done.1 = f32[3,1,64,256]{3,2,1,0:T(8,128)} collective-permute-done((f32[3,1,64,256]{3,2,1,0:T(8,128)}, f32[3,1,64,256]{3,2,1,0:T(8,128)}, u32[]{:S(2)}, u32[]{:S(2)}) %collective-permute-start.1) | collective-permute-done | bytes 196640 | tf_op jit(solution)/shard_map/ppermute | solution.py:23
  66.5 1.7 constant_dynamic-update-slice_fusion.2
  68.2 2.5 constant_dynamic-update-slice_fusion.1
  70.8 1.8 constant_dynamic-update-slice_fusion
  74.2 3.5 %concatenate.72 = bf16[3,16,64,2,128]{4,3,2,1,0:T(2,128)(2,1)} reshape(bf16[3,16,64,256]{3,2,1,0:T(8,128)(2,1)} %get-tuple-element.21) | data formatting | bytes 3145728 | tf_op jit(solution)/shard_map/concatenate | solution.py:27
  77.7 4.4 %copy.130 = bf16[3,16,64,2,128]{4,1,3,2,0:T(8,128)(2,1)} copy(bf16[3,16,64,2,128]{4,3,2,1,0:T(2,128)(2,1)} %concatenate.72) | data formatting | bytes 3145728 | tf_op jit(solution)/shard_map/concatenate | solution.py:27
  82.8 5.6 %bitcast_convert_fusion.1 = bf16[16,2,8,3,64,128]{5,2,4,3,1,0:T(8,128)(2,1)S(1)} fusion(bf16[3,1,64,2,128]{4,1,3,2,0:T(2,128)(2,1)} %concatenate.87, bf16[3,16,64,2,128]{4,1,3,2,0:T(8,128)(2,1)} %copy.130, bf16[3,1,64,2,128]{4,1,3,2,0:T(2,128)(2,1)} %concatenate.86, s32[18,2]{0,1:T(2,128)S(1)} %multiply_add_fusion, s32[16,2,8]{2,1,0:T(2,128)S(1)} %bitcast.122), kind=kOutput, calls=%fused_computation.1 | convolution fusion | flops 464593920 | bytes 14353552 | tf_op jit(solution)/shard_map/xbkqc,aqycz->xbkayz/dot_general | solution.py:117
  88.4 3.4 %fusion.14 = f32[3,16,64,2,128]{4,2,0,3,1:T(8,128)S(1)} fusion(bf16[16,2,8,3,64,128]{5,2,4,3,1,0:T(8,128)(2,1)S(1)} %bitcast_convert_fusion.1, bf16[8,128,128]{2,1,0:T(8,128)(2,1)S(1)} %copy-done), kind=kOutput, calls=%fused_computation.40 | convolution fusion | flops 1610612736 | bytes 15990784 | tf_op jit(solution)/shard_map/xbkayz,kzw->axybw/dot_general | solution.py:120
  91.8 4.4 %copy.133 = f32[3,16,64,2,128]{4,3,2,1,0:T(2,128)} copy(f32[3,16,64,2,128]{4,2,0,3,1:T(8,128)S(1)} %fusion.14) | data formatting | bytes 6291456 | tf_op jit(solution)/shard_map/xbkayz,kzw->axybw/transpose | solution.py:120
  96.2 5.5 %reshape.196 = f32[3,16,64,256]{3,2,1,0:T(8,128)} reshape(f32[3,16,64,2,128]{4,3,2,1,0:T(2,128)} %copy.133) | data formatting | bytes 6291456 | tf_op jit(solution)/shard_map/reshape | solution.py:123
  101.8 1.9 fusion.62
  103.7 3.0 collective-permute-start.2
  106.7 10.1 %all-to-all-start.1 = ((bf16[128,2,3,2048]{3,1,2,0:T(2,128)(2,1)}), bf16[128,2,3,2048]{3,1,2,0:T(2,128)(2,1)}, u32[]{:S(2)}, u32[]{:S(2)}) async-start(bf16[128,2,3,2048]{3,1,2,0:T(2,128)(2,1)} %copy.136), calls=%async_computation.1 | async-start | bytes 6291456 | tf_op jit(solution)/shard_map/all_to_all | solution.py:176
  116.8 5.8 %copy.122 = bf16[128,2,3,2048]{3,1,0,2:T(2,128)(2,1)} copy(bf16[128,2,3,2048]{3,1,2,0:T(2,128)(2,1)} %all-to-all-done) | data formatting | bytes 6291456 | tf_op jit(solution)/shard_map/all_to_all | solution.py:176
  122.7 5.7 %reshape.195 = bf16[256,3,2048]{2,0,1:T(8,128)(2,1)} reshape(bf16[128,2,3,2048]{3,1,0,2:T(2,128)(2,1)} %copy.122) | data formatting | bytes 6291456 | tf_op jit(solution)/shard_map/reshape | solution.py:183
  128.4 4.0 %fusion.4 = (f32[2048,128]{1,0:T(8,128)}, bf16[3,2048,128]{2,1,0:T(8,128)(2,1)S(1)}) fusion(bf16[256,3,2048]{2,0,1:T(8,128)(2,1)} %reshape.195, s32[128]{0:T(128)S(1)} %copy-done.8), kind=kOutput, calls=%fused_computation.12 | convolution fusion | flops 405569536 | bytes 5767680 | tf_op jit(solution)/shard_map/jr,rcb->cjb/dot_general | solution.py:184
  132.6 2.1 slice_multiply_fusion.3
  134.7 2.5 copy.124
  137.2 2.4 mul.349
  139.6 2.5 multiply_bitcast_fusion.1
  142.1 3.8 %bitcast_multiply_fusion.1 = (f32[16,64,256]{2,1,0:T(8,128)}, f32[16,64,256]{2,1,0:T(8,128)}) fusion(f32[16,64,256]{2,1,0:T(8,128)} %mul.349, f32[3,16,64,256]{3,2,1,0:T(8,128)S(1)} %copy-done.1, f32[16,64,80]{2,1,0:T(8,128)} %bitcast.121, f32[80]{0:T(128)S(1)} %get-tuple-element.30), kind=kOutput, calls=%fused_computation.52 | convolution fusion | flops 252526592 | bytes 4522304 | tf_op jit(solution)/shard_map/dot_general | solution.py:65
  145.9 1.6 copy.125
  151.6 14.2 %fusion.61 = (bf16[3,16,64,256]{3,2,1,0:T(8,128)(2,1)}, f32[3,16,64,256]{3,2,1,0:T(8,128)S(1)}) fusion(f32[16]{0:T(128)S(1)} %broadcast_select_fusion, f32[16,64,256]{2,1,0:T(8,128)} %get-tuple-element.35, f32[3]{0:T(128)S(1)} %compare_convert_fusion, f32[3,16,64,256]{3,2,1,0:T(8,128)} %param.11, f32[3,16,64,256]{3,2,1,0:T(8,128)} %reshape.196, ...), kind=kLoop, calls=%fused_computation.120 | loop fusion | flops 23592960 | bytes 26562636 | tf_op jit(solution)/shard_map/convert.6
  166.6 3.8 %fusion.63 = (f32[3,16,64,255]{3,2,1,0:T(8,128)}, f32[3,16,64,255]{3,2,1,0:T(8,128)}) fusion(f32[3,16,64,256]{3,2,1,0:T(8,128)S(1)} %get-tuple-element.3), kind=kLoop, calls=%fused_computation.122 | loop fusion | bytes 12533760 | tf_op jit(solution)/shard_map/slice | solution.py:96
  170.4 5.8 %copy.137 = bf16[128,2,3,2048]{3,1,0,2:T(2,128)(2,1)} copy(bf16[128,2,3,2048]{3,1,2,0:T(2,128)(2,1)} %all-to-all-done.1) | data formatting | bytes 6291456 | tf_op jit(solution)/shard_map/all_to_all | solution.py:176
  176.2 5.7 %reshape.198 = bf16[256,3,2048]{2,0,1:T(8,128)(2,1)} reshape(bf16[128,2,3,2048]{3,1,0,2:T(2,128)(2,1)} %copy.137) | data formatting | bytes 6291456 | tf_op jit(solution)/shard_map/reshape | solution.py:183
  181.9 4.0 %fusion.5 = (f32[2048,128]{1,0:T(8,128)}, bf16[3,2048,128]{2,1,0:T(8,128)(2,1)S(1)}) fusion(bf16[256,3,2048]{2,0,1:T(8,128)(2,1)} %reshape.198, s32[128]{0:T(128)S(1)} %copy-done.8), kind=kOutput, calls=%fused_computation.13 | convolution fusion | flops 405569536 | bytes 5767680 | tf_op jit(solution)/shard_map/jr,rcb->cjb/dot_general | solution.py:184
  186.2 2.3 slice_multiply_fusion.2
  188.4 2.5 copy.149
  191.0 2.4 mul.428
  196.0 2.5 copy.148
  198.6 2.4 mul.422
  200.9 1.7 slice_multiply_fusion.1
  204.0 67.2 %psum.16 = f32[80]{0:T(128)S(1)} all-reduce(f32[80]{0:T(128)S(1)} %select_add_fusion), channel_id=1, replica_groups=mesh['gx'=64,'gy'=2] {'gx','gy'}, use_global_device_ids=true, to_apply=%region_6.7 | all-reduce | flops 80 | bytes 640 | tf_op jit(solution)/shard_map/psum | solution.py:200
  272.0 2.4 collective-permute-start.5
  274.4 2.5 copy.139
  277.0 2.4 mul.395
  279.3 2.5 multiply_bitcast_fusion
  281.9 2.7 bitcast_multiply_fusion
  284.6 3.5 %concatenate.83 = bf16[3,16,64,2,128]{4,3,2,1,0:T(2,128)(2,1)} reshape(bf16[3,16,64,256]{3,2,1,0:T(8,128)(2,1)} %get-tuple-element.2) | data formatting | bytes 3145728 | tf_op jit(solution)/shard_map/concatenate | solution.py:27
  288.1 4.4 %copy.144 = bf16[3,16,64,2,128]{4,1,3,2,0:T(8,128)(2,1)} copy(bf16[3,16,64,2,128]{4,3,2,1,0:T(2,128)(2,1)} %concatenate.83) | data formatting | bytes 3145728 | tf_op jit(solution)/shard_map/concatenate | solution.py:27
  292.5 2.5 copy.140
  295.0 2.4 mul.398
  297.4 2.5 copy.141
  299.9 2.4 mul.401
  302.3 2.5 copy.142
  304.8 2.4 mul.409
  314.1 5.6 %bitcast_convert_fusion = bf16[16,2,8,3,64,128]{5,2,4,3,1,0:T(8,128)(2,1)S(1)} fusion(bf16[3,1,64,2,128]{4,1,3,2,0:T(2,128)(2,1)} %concatenate.89, bf16[3,16,64,2,128]{4,1,3,2,0:T(8,128)(2,1)} %copy.144, bf16[3,1,64,2,128]{4,1,3,2,0:T(2,128)(2,1)} %concatenate.88, s32[18,2]{0,1:T(2,128)S(1)} %multiply_add_fusion, s32[16,2,8]{2,1,0:T(2,128)S(1)} %bitcast.123), kind=kOutput, calls=%fused_computation | convolution fusion | flops 464593920 | bytes 14353552 | tf_op jit(solution)/shard_map/xbkqc,aqycz->xbkayz/dot_general | solution.py:117
  319.7 3.4 %fusion.17 = f32[3,16,64,2,128]{4,2,0,3,1:T(8,128)S(1)} fusion(bf16[16,2,8,3,64,128]{5,2,4,3,1,0:T(8,128)(2,1)S(1)} %bitcast_convert_fusion, bf16[8,128,128]{2,1,0:T(8,128)(2,1)S(1)} %copy-done), kind=kOutput, calls=%fused_computation.41 | convolution fusion | flops 1610612736 | bytes 15990784 | tf_op jit(solution)/shard_map/xbkayz,kzw->axybw/dot_general | solution.py:120
  323.1 4.4 %copy.147 = f32[3,16,64,2,128]{4,3,2,1,0:T(2,128)} copy(f32[3,16,64,2,128]{4,2,0,3,1:T(8,128)S(1)} %fusion.17) | data formatting | bytes 6291456 | tf_op jit(solution)/shard_map/xbkayz,kzw->axybw/transpose | solution.py:120
  327.6 5.5 %reshape.199 = f32[3,16,64,256]{3,2,1,0:T(8,128)} reshape(f32[3,16,64,2,128]{4,3,2,1,0:T(2,128)} %copy.147) | data formatting | bytes 6291456 | tf_op jit(solution)/shard_map/reshape | solution.py:123
  333.1 9.4 %subtract_multiply_fusion = f32[3,16,64,256]{3,2,1,0:T(8,128)} fusion(f32[3,16,64,256]{3,2,1,0:T(8,128)S(1)} %get-tuple-element.3, f32[3,16,64,256]{3,2,1,0:T(8,128)} %reshape.199, f32[3,16,64,255]{3,2,1,0:T(8,128)} %get-tuple-element.17, f32[3,16,64,255]{3,2,1,0:T(8,128)} %get-tuple-element.16, f32[3,18,1,256]{3,2,1,0:T(1,128)} %collective-permute-done.6, ...), kind=kLoop, calls=%fused_computation.26 | loop fusion | flops 25952256 | bytes 21450828 | tf_op jit(solution)/shard_map/mul | solution.py:128
  (81 shorter events, 24.4 us)
Async XLA Ops:
  0.6 87.7 %copy-start = (bf16[8,128,128]{2,1,0:T(8,128)(2,1)S(1)}, bf16[8,128,128]{2,1,0:T(8,128)(2,1)}, u32[]{:S(2)}) copy-start(bf16[8,128,128]{2,1,0:T(8,128)(2,1)} %param.16) | copy-start | bytes 786436
  15.6 11.9 %copy-start.1 = (f32[3,16,64,256]{3,2,1,0:T(8,128)S(1)}, f32[3,16,64,256]{3,2,1,0:T(8,128)}, u32[]{:S(2)}) copy-start(f32[3,16,64,256]{3,2,1,0:T(8,128)} %param.11) | copy-start | bytes 9437188
  15.6 91.2 %all-to-all-start = ((bf16[128,2,3,2048]{3,1,2,0:T(2,128)(2,1)}), bf16[128,2,3,2048]{3,1,2,0:T(2,128)(2,1)}, u32[]{:S(2)}, u32[]{:S(2)}) async-start(bf16[128,2,3,2048]{3,1,2,0:T(2,128)(2,1)} %copy.121), calls=%async_computation | async-start | bytes 6291456 | tf_op jit(solution)/shard_map/all_to_all | solution.py:176
  28.3 38.3 %collective-permute-start.1 = (f32[3,1,64,256]{3,2,1,0:T(8,128)}, f32[3,1,64,256]{3,2,1,0:T(8,128)}, u32[]{:S(2)}, u32[]{:S(2)}) collective-permute-start(f32[3,1,64,256]{3,2,1,0:T(8,128)} %get-tuple-element.24), channel_id=1, source_target_pairs={{0,2},{2,4},{4,6},{6,8},{8,10},{10,12},{12,14},{14,16},{16,18},{18... | collective-permute-start | bytes 589832 | tf_op jit(solution)/shard_map/ppermute | solution.py:23
  31.8 39.0 %collective-permute-start = (f32[3,1,64,256]{3,2,1,0:T(8,128)}, f32[3,1,64,256]{3,2,1,0:T(8,128)}, u32[]{:S(2)}, u32[]{:S(2)}) collective-permute-start(f32[3,1,64,256]{3,2,1,0:T(8,128)} %get-tuple-element.25), channel_id=1, source_target_pairs={{2,0},{4,2},{6,4},{8,6},{10,8},{12,10},{14,12},{16,14},{18,16},{20... | collective-permute-start | bytes 589832 | tf_op jit(solution)/shard_map/ppermute | solution.py:26
  32.0 3.8 %copy-start.6 = (bf16[2,128,3,2048]{3,1,2,0:T(8,128)(2,1)S(1)}, bf16[2,128,3,2048]{3,1,2,0:T(8,128)(2,1)}, u32[]{:S(2)}) copy-start(bf16[2,128,3,2048]{3,1,2,0:T(8,128)(2,1)} %param.12) | copy-start | bytes 9437188
  35.8 2.7 copy-start.11
  35.8 6.0 %copy-start.12 = (f32[80]{0:T(128)S(1)}, f32[80]{0:T(128)}, u32[]{:S(2)}) copy-start(f32[80]{0:T(128)} %param.18) | copy-start | bytes 964
  35.8 6.0 %copy-start.9 = (s32[80]{0:T(128)S(1)}, s32[80]{0:T(128)}, u32[]{:S(2)}) copy-start(s32[80]{0:T(128)} %param.20) | copy-start | bytes 964
  35.8 6.0 %copy-start.10 = (f32[80]{0:T(128)S(1)}, f32[80]{0:T(128)}, u32[]{:S(2)}) copy-start(f32[80]{0:T(128)} %param.17) | copy-start | bytes 964
  35.8 9.8 %copy-start.7 = (s32[32,8]{0,1:T(8,128)S(1)}, s32[32,8]{0,1:T(8,128)}, u32[]{:S(2)}) copy-start(s32[32,8]{0,1:T(8,128)} %param.15) | copy-start | bytes 3076
  51.7 5.7 %copy-start.13 = (s32[128]{0:T(128)S(1)}, s32[128]{0:T(128)}, u32[]{:S(2)}) copy-start(s32[128]{0:T(128)} %param.21) | copy-start | bytes 1540
  103.7 48.0 %collective-permute-start.2 = (f32[3,18,1,256]{3,2,1,0:T(1,128)}, f32[3,18,1,256]{3,2,1,0:T(1,128)S(1)}, u32[]{:S(2)}, u32[]{:S(2)}) collective-permute-start(f32[3,18,1,256]{3,2,1,0:T(1,128)} %get-tuple-element.6), channel_id=1, source_target_pairs={{1,0},{0,1},{3,2},{2,3},{5,4},{4,5},{7,6},{6,7},{9,8},{8,9},{11,10... | collective-permute-start | bytes 165896 | tf_op jit(solution)/shard_map/ppermute | solution.py:26
  106.7 44.9 %collective-permute-start.3 = (f32[3,18,1,256]{3,2,1,0:T(1,128)}, f32[3,18,1,256]{3,2,1,0:T(1,128)}, u32[]{:S(2)}, u32[]{:S(2)}) collective-permute-start(f32[3,18,1,256]{3,2,1,0:T(1,128)} %get-tuple-element.7), channel_id=1, source_target_pairs={{0,1},{1,0},{2,3},{3,2},{4,5},{5,4},{6,7},{7,6},{8,9},{9,8},{10,11... | collective-permute-start | bytes 165896 | tf_op jit(solution)/shard_map/ppermute | solution.py:23
  106.7 63.7 %all-to-all-start.1 = ((bf16[128,2,3,2048]{3,1,2,0:T(2,128)(2,1)}), bf16[128,2,3,2048]{3,1,2,0:T(2,128)(2,1)}, u32[]{:S(2)}, u32[]{:S(2)}) async-start(bf16[128,2,3,2048]{3,1,2,0:T(2,128)(2,1)} %copy.136), calls=%async_computation.1 | async-start | bytes 6291456 | tf_op jit(solution)/shard_map/all_to_all | solution.py:176
  122.7 5.7 %copy-start.8 = (s32[128]{0:T(128)S(1)}, s32[128]{0:T(128)}, u32[]{:S(2)}) copy-start(s32[128]{0:T(128)} %param.14) | copy-start | bytes 1540
  145.9 2.8 copy-start.4
  147.5 2.6 copy-start.5
  193.3 1.4 copy-start.2
  200.9 1.7 copy-start.3
  271.2 36.7 %collective-permute-start.4 = (f32[3,1,64,256]{3,2,1,0:T(8,128)}, f32[3,1,64,256]{3,2,1,0:T(8,128)}, u32[]{:S(2)}, u32[]{:S(2)}) collective-permute-start(f32[3,1,64,256]{3,2,1,0:T(8,128)} %get-tuple-element.19), channel_id=1, source_target_pairs={{2,0},{4,2},{6,4},{8,6},{10,8},{12,10},{14,12},{16,14},{18,16},{20... | collective-permute-start | bytes 589832 | tf_op jit(solution)/shard_map/ppermute | solution.py:26
  272.0 35.8 %collective-permute-start.5 = (f32[3,1,64,256]{3,2,1,0:T(8,128)}, f32[3,1,64,256]{3,2,1,0:T(8,128)}, u32[]{:S(2)}, u32[]{:S(2)}) collective-permute-start(f32[3,1,64,256]{3,2,1,0:T(8,128)} %get-tuple-element.18), channel_id=1, source_target_pairs={{0,2},{2,4},{4,6},{6,8},{8,10},{10,12},{12,14},{14,16},{16,18},{18... | collective-permute-start | bytes 589832 | tf_op jit(solution)/shard_map/ppermute | solution.py:23
  309.3 23.7 %collective-permute-start.6 = (f32[3,18,1,256]{3,2,1,0:T(1,128)}, f32[3,18,1,256]{3,2,1,0:T(1,128)}, u32[]{:S(2)}, u32[]{:S(2)}) collective-permute-start(f32[3,18,1,256]{3,2,1,0:T(1,128)} %get-tuple-element.5), channel_id=1, source_target_pairs={{1,0},{0,1},{3,2},{2,3},{5,4},{4,5},{7,6},{6,7},{9,8},{8,9},{11,10... | collective-permute-start | bytes 165896 | tf_op jit(solution)/shard_map/ppermute | solution.py:26
  309.3 23.7 %collective-permute-start.7 = (f32[3,18,1,256]{3,2,1,0:T(1,128)}, f32[3,18,1,256]{3,2,1,0:T(1,128)}, u32[]{:S(2)}, u32[]{:S(2)}) collective-permute-start(f32[3,18,1,256]{3,2,1,0:T(1,128)} %get-tuple-element.4), channel_id=1, source_target_pairs={{0,1},{1,0},{2,3},{3,2},{4,5},{5,4},{6,7},{7,6},{8,9},{9,8},{10,11... | collective-permute-start | bytes 165896 | tf_op jit(solution)/shard_map/ppermute | solution.py:23
where the time goes:
time: 349 us; the launch traced here: 343 us
  local copies, waits for them, and re-layouts  138 us (40%)
  blocking collectives  67.2 us (19%)
  other arithmetic  54.9 us (16%)
  matrix products  39 us (11%)
  starting transfers between devices  33.5 us (10%)
  waiting for transfers between devices  8.97 us (3%)
    psum x1, blocking collectives, shards(): gradient_sum = gradient_sum + lax.psum(gradient_part, ('gx', 'gy'))  67.2 us
    all_to_all x2, starting transfers between devices, shards(): lax.all_to_all(packed.reshape((tile_count, CAP) + block_shape), ('gx', 'g...  22 us
    reshape x4, local copies, waits for them, and re-layouts, shards(): packed.reshape((tile_count, CAP) + block_shape)  20.1 us
    concatenate x8, local copies, waits for them, and re-layouts, padded(): block = jnp.concatenate([low, block, high], axis=dim)  19.5 us
    another operation x3, other arithmetic  16.1 us
    all_to_all x2, local copies, waits for them, and re-layouts, shards(): lax.all_to_all(packed.reshape((tile_count, CAP) + block_shape), ('gx', 'g...  11.7 us
    reshape x2, local copies, waits for them, and re-layouts, shards(): arrived = arrived.reshape((tile_count * CAP,) + block_shape)  11.4 us
    dot_general x2, matrix products, advance(): jnp.einsum('xbkqc,aqycz->xbkayz', selector, planes, preferred_element_typ...  11.2 us
  transfers between devices with their start and end apart: 10, of which 1 were waited for; matrix products, arithmetic and copies ran while one was open for 50% of the time, Pallas kernels for 0%

commit v1 on v0

--- a/solution.py
+++ b/solution.py
@@ -197,7 +197,7 @@
             drag_field,
             fringe_scale,
         )
-        gradient_sum = gradient_sum + lax.psum(gradient_part, ("gx", "gy"))
+        gradient_sum = gradient_sum + lax.psum(lax.psum(gradient_part, "gy"), "gx")
     cosine = jnp.cos(yaw_angle)
     sine = jnp.sin(yaw_angle)
     control_gradient = jnp.stack(

time: 349 us -> 453 us (1.30)
  blocking collectives: 67.2 us -> 168 us
    psum x1 -> x2, blocking collectives: 67.2 us -> 168 us  [shards(): gradient_sum = gradient_sum + lax.psum(lax.psum(gradient_part, 'gy'), 'gx')]
    ppermute x4, starting transfers between devices: 4.07 us -> 10.5 us  [padded(): lax.ppermute(lax.slice_in_dim(block, 0, width, axis=dim), axis, backward)]
  transfers between devices with their start and end apart: 10 -> 10, of which waited for: 1 -> 1; matrix products, arithmetic and copies ran while one was open for 50% -> 39% of each run, Pallas kernels for 0% -> 0%
where the time goes in v1:
time: 453 us; the launch traced here: 447 us
  blocking collectives  168 us (37%)
  local copies, waits for them, and re-layouts  138 us (30%)
  other arithmetic  54.9 us (12%)
  matrix products  39 us (9%)
  starting transfers between devices  37 us (8%)
  waiting for transfers between devices  8.89 us (2%)
    psum x2, blocking collectives, shards(): gradient_sum = gradient_sum + lax.psum(lax.psum(gradient_part, 'gy'), 'gx')  168 us
    all_to_all x2, starting transfers between devices, shards(): lax.all_to_all(packed.reshape((tile_count, CAP) + block_shape), ('gx', 'g...  22 us
    reshape x4, local copies, waits for them, and re-layouts, shards(): packed.reshape((tile_count, CAP) + block_shape)  20.1 us
    concatenate x8, local copies, waits for them, and re-layouts, padded(): block = jnp.concatenate([low, block, high], axis=dim)  19.5 us
    another operation x3, other arithmetic  16 us
    all_to_all x2, local copies, waits for them, and re-layouts, shards(): lax.all_to_all(packed.reshape((tile_count, CAP) + block_shape), ('gx', 'g...  11.7 us
    reshape x2, local copies, waits for them, and re-layouts, shards(): arrived = arrived.reshape((tile_count * CAP,) + block_shape)  11.4 us
    dot_general x2, matrix products, advance(): jnp.einsum('xbkqc,aqycz->xbkayz', selector, planes, preferred_element_typ...  11.2 us
  transfers between devices with their start and end apart: 10, of which 1 were waited for; matrix products, arithmetic and copies ran while one was open for 39% of the time, Pallas kernels for 0%

profile of v1, /device:TPU:1, one launch (start us, length us, event | category | flops | bytes accessed | tf_op | source)
XLA Modules:
  0.0 446.8 jit_solution(10351420911042665298)
XLA Ops:
  3.1 4.0 convolution_convert_fusion.1
  7.1 4.6 %reshape.194 = bf16[128,2,3,2048]{3,1,0,2:T(2,128)(2,1)S(1)} reshape(bf16[256,3,2048]{2,0,1:T(8,128)(2,1)} %convolution_convert_fusion.1) | data formatting | bytes 6291456 | tf_op jit(solution)/shard_map/reshape | solution.py:177
  11.7 3.8 copy.121
  15.6 11.9 %all-to-all-start = ((bf16[128,2,3,2048]{3,1,2,0:T(2,128)(2,1)}), bf16[128,2,3,2048]{3,1,2,0:T(2,128)(2,1)}, u32[]{:S(2)}, u32[]{:S(2)}) async-start(bf16[128,2,3,2048]{3,1,2,0:T(2,128)(2,1)} %copy.121), calls=%async_computation | async-start | bytes 6291456 | tf_op jit(solution)/shard_map/all_to_all | solution.py:176
  28.3 3.5 collective-permute-start.1
  32.0 3.8 fusion.65
  35.9 2.6 convolution_convert_fusion
  39.8 2.0 mul.377
  41.9 1.8 multiply_bitcast_fusion.2
  43.7 2.0 copy.160
  45.7 6.0 %reshape.197 = bf16[128,2,3,2048]{3,1,0,2:T(2,128)(2,1)} reshape(bf16[256,3,2048]{2,0,1:T(8,128)(2,1)} %convolution_convert_fusion) | data formatting | bytes 6291456 | tf_op jit(solution)/shard_map/reshape | solution.py:177
  51.8 5.7 %copy.136 = bf16[128,2,3,2048]{3,1,2,0:T(2,128)(2,1)} copy(bf16[128,2,3,2048]{3,1,0,2:T(2,128)(2,1)} %reshape.197) | data formatting | bytes 6291456 | tf_op jit(solution)/shard_map/reshape | solution.py:177
  57.7 8.9 %collective-permute-done.1 = f32[3,1,64,256]{3,2,1,0:T(8,128)} collective-permute-done((f32[3,1,64,256]{3,2,1,0:T(8,128)}, f32[3,1,64,256]{3,2,1,0:T(8,128)}, u32[]{:S(2)}, u32[]{:S(2)}) %collective-permute-start.1) | collective-permute-done | bytes 196640 | tf_op jit(solution)/shard_map/ppermute | solution.py:23
  66.5 1.7 constant_dynamic-update-slice_fusion.2
  68.3 2.5 constant_dynamic-update-slice_fusion.1
  70.8 1.8 constant_dynamic-update-slice_fusion
  74.2 3.5 concatenate.72
  77.7 4.4 copy.130
  82.8 5.6 %bitcast_convert_fusion.1 = bf16[16,2,8,3,64,128]{5,2,4,3,1,0:T(8,128)(2,1)S(1)} fusion(bf16[3,1,64,2,128]{4,1,3,2,0:T(2,128)(2,1)} %concatenate.87, bf16[3,16,64,2,128]{4,1,3,2,0:T(8,128)(2,1)} %copy.130, bf16[3,1,64,2,128]{4,1,3,2,0:T(2,128)(2,1)} %concatenate.86, s32[18,2]{0,1:T(2,128)S(1)} %multiply_add_fusion, s32[16,2,8]{2,1,0:T(2,128)S(1)} %bitcast.122), kind=kOutput, calls=%fused_computation.1 | convolution fusion | flops 464593920 | bytes 14353552 | tf_op jit(solution)/shard_map/xbkqc,aqycz->xbkayz/dot_general | solution.py:117
  88.4 3.4 fusion.14
  91.9 4.4 copy.133
  96.3 5.5 %reshape.196 = f32[3,16,64,256]{3,2,1,0:T(8,128)} reshape(f32[3,16,64,2,128]{4,3,2,1,0:T(2,128)} %copy.133) | data formatting | bytes 6291456 | tf_op jit(solution)/shard_map/reshape | solution.py:123
  101.9 1.9 fusion.62
  103.7 3.0 collective-permute-start.2
  106.8 10.1 %all-to-all-start.1 = ((bf16[128,2,3,2048]{3,1,2,0:T(2,128)(2,1)}), bf16[128,2,3,2048]{3,1,2,0:T(2,128)(2,1)}, u32[]{:S(2)}, u32[]{:S(2)}) async-start(bf16[128,2,3,2048]{3,1,2,0:T(2,128)(2,1)} %copy.136), calls=%async_computation.1 | async-start | bytes 6291456 | tf_op jit(solution)/shard_map/all_to_all | solution.py:176
  116.9 5.8 %copy.122 = bf16[128,2,3,2048]{3,1,0,2:T(2,128)(2,1)} copy(bf16[128,2,3,2048]{3,1,2,0:T(2,128)(2,1)} %all-to-all-done) | data formatting | bytes 6291456 | tf_op jit(solution)/shard_map/all_to_all | solution.py:176
  122.8 5.7 %reshape.195 = bf16[256,3,2048]{2,0,1:T(8,128)(2,1)} reshape(bf16[128,2,3,2048]{3,1,0,2:T(2,128)(2,1)} %copy.122) | data formatting | bytes 6291456 | tf_op jit(solution)/shard_map/reshape | solution.py:183
  128.5 4.0 fusion.4
  132.7 2.1 slice_multiply_fusion.3
  134.8 2.5 copy.124
  137.3 2.4 mul.349
  139.7 2.5 multiply_bitcast_fusion.1
  142.2 3.8 bitcast_multiply_fusion.1
  151.7 14.2 %fusion.61 = (bf16[3,16,64,256]{3,2,1,0:T(8,128)(2,1)}, f32[3,16,64,256]{3,2,1,0:T(8,128)S(1)}) fusion(f32[16]{0:T(128)S(1)} %broadcast_select_fusion, f32[16,64,256]{2,1,0:T(8,128)} %get-tuple-element.35, f32[3]{0:T(128)S(1)} %compare_convert_fusion, f32[3,16,64,256]{3,2,1,0:T(8,128)} %param.11, f32[3,16,64,256]{3,2,1,0:T(8,128)} %reshape.196, ...), kind=kLoop, calls=%fused_computation.120 | loop fusion | flops 23592960 | bytes 26562636 | tf_op jit(solution)/shard_map/convert.6
  166.7 3.8 fusion.63
  170.5 5.8 %copy.137 = bf16[128,2,3,2048]{3,1,0,2:T(2,128)(2,1)} copy(bf16[128,2,3,2048]{3,1,2,0:T(2,128)(2,1)} %all-to-all-done.1) | data formatting | bytes 6291456 | tf_op jit(solution)/shard_map/all_to_all | solution.py:176
  176.3 5.7 %reshape.198 = bf16[256,3,2048]{2,0,1:T(8,128)(2,1)} reshape(bf16[128,2,3,2048]{3,1,0,2:T(2,128)(2,1)} %copy.137) | data formatting | bytes 6291456 | tf_op jit(solution)/shard_map/reshape | solution.py:183
  182.0 4.0 fusion.5
  186.2 2.3 slice_multiply_fusion.2
  188.5 2.5 copy.149
  191.0 2.4 mul.428
  196.1 2.5 copy.148
  198.6 2.4 mul.422
  201.0 1.7 slice_multiply_fusion.1
  204.0 3.8 psum.33
  207.8 164.0 %psum.32 = f32[80]{0:T(128)S(1)} all-reduce(f32[80]{0:T(128)S(1)} %psum.33), channel_id=1, replica_groups=mesh['gx'=64,'gy'=2] {'gx'}, use_global_device_ids=true, to_apply=%region_7.8 | all-reduce | flops 80 | bytes 640 | tf_op jit(solution)/shard_map/psum | solution.py:200
  371.8 6.7 %collective-permute-start.4 = (f32[3,1,64,256]{3,2,1,0:T(8,128)}, f32[3,1,64,256]{3,2,1,0:T(8,128)}, u32[]{:S(2)}, u32[]{:S(2)}) collective-permute-start(f32[3,1,64,256]{3,2,1,0:T(8,128)} %get-tuple-element.19), channel_id=1, source_target_pairs={{2,0},{4,2},{6,4},{8,6},{10,8},{12,10},{14,12},{16,14},{18,16},{20... | collective-permute-start | bytes 589832 | tf_op jit(solution)/shard_map/ppermute | solution.py:26
  378.6 2.5 copy.139
  381.1 2.4 mul.395
  383.5 2.5 multiply_bitcast_fusion
  386.0 2.7 bitcast_multiply_fusion
  388.8 3.5 concatenate.83
  392.3 4.4 copy.144
  396.6 2.5 copy.140
  399.2 2.3 mul.398
  401.5 2.5 copy.141
  404.1 2.3 mul.401
  406.4 2.5 copy.142
  408.9 2.4 mul.409
  418.2 5.6 %bitcast_convert_fusion = bf16[16,2,8,3,64,128]{5,2,4,3,1,0:T(8,128)(2,1)S(1)} fusion(bf16[3,1,64,2,128]{4,1,3,2,0:T(2,128)(2,1)} %concatenate.89, bf16[3,16,64,2,128]{4,1,3,2,0:T(8,128)(2,1)} %copy.144, bf16[3,1,64,2,128]{4,1,3,2,0:T(2,128)(2,1)} %concatenate.88, s32[18,2]{0,1:T(2,128)S(1)} %multiply_add_fusion, s32[16,2,8]{2,1,0:T(2,128)S(1)} %bitcast.123), kind=kOutput, calls=%fused_computation | convolution fusion | flops 464593920 | bytes 14353552 | tf_op jit(solution)/shard_map/xbkqc,aqycz->xbkayz/dot_general | solution.py:117
  423.8 3.4 fusion.17
  427.3 4.4 copy.147
  431.7 5.5 %reshape.199 = f32[3,16,64,256]{3,2,1,0:T(8,128)} reshape(f32[3,16,64,2,128]{4,3,2,1,0:T(2,128)} %copy.147) | data formatting | bytes 6291456 | tf_op jit(solution)/shard_map/reshape | solution.py:123
  437.2 9.4 %subtract_multiply_fusion = f32[3,16,64,256]{3,2,1,0:T(8,128)} fusion(f32[3,16,64,256]{3,2,1,0:T(8,128)S(1)} %get-tuple-element.3, f32[3,16,64,256]{3,2,1,0:T(8,128)} %reshape.199, f32[3,16,64,255]{3,2,1,0:T(8,128)} %get-tuple-element.17, f32[3,16,64,255]{3,2,1,0:T(8,128)} %get-tuple-element.16, f32[3,18,1,256]{3,2,1,0:T(1,128)} %collective-permute-done.6, ...), kind=kLoop, calls=%fused_computation.26 | loop fusion | flops 25952256 | bytes 21450828 | tf_op jit(solution)/shard_map/mul | solution.py:128
  (82 shorter events, 25.2 us)
Async XLA Ops:
  0.6 87.8 %copy-start = (bf16[8,128,128]{2,1,0:T(8,128)(2,1)S(1)}, bf16[8,128,128]{2,1,0:T(8,128)(2,1)}, u32[]{:S(2)}) copy-start(bf16[8,128,128]{2,1,0:T(8,128)(2,1)} %param.16) | copy-start | bytes 786436
  15.6 11.9 %copy-start.1 = (f32[3,16,64,256]{3,2,1,0:T(8,128)S(1)}, f32[3,16,64,256]{3,2,1,0:T(8,128)}, u32[]{:S(2)}) copy-start(f32[3,16,64,256]{3,2,1,0:T(8,128)} %param.11) | copy-start | bytes 9437188
  15.6 91.3 %all-to-all-start = ((bf16[128,2,3,2048]{3,1,2,0:T(2,128)(2,1)}), bf16[128,2,3,2048]{3,1,2,0:T(2,128)(2,1)}, u32[]{:S(2)}, u32[]{:S(2)}) async-start(bf16[128,2,3,2048]{3,1,2,0:T(2,128)(2,1)} %copy.121), calls=%async_computation | async-start | bytes 6291456 | tf_op jit(solution)/shard_map/all_to_all | solution.py:176
  28.3 38.2 %collective-permute-start.1 = (f32[3,1,64,256]{3,2,1,0:T(8,128)}, f32[3,1,64,256]{3,2,1,0:T(8,128)}, u32[]{:S(2)}, u32[]{:S(2)}) collective-permute-start(f32[3,1,64,256]{3,2,1,0:T(8,128)} %get-tuple-element.24), channel_id=1, source_target_pairs={{0,2},{2,4},{4,6},{6,8},{8,10},{10,12},{12,14},{14,16},{16,18},{18... | collective-permute-start | bytes 589832 | tf_op jit(solution)/shard_map/ppermute | solution.py:23
  31.8 39.0 %collective-permute-start = (f32[3,1,64,256]{3,2,1,0:T(8,128)}, f32[3,1,64,256]{3,2,1,0:T(8,128)}, u32[]{:S(2)}, u32[]{:S(2)}) collective-permute-start(f32[3,1,64,256]{3,2,1,0:T(8,128)} %get-tuple-element.25), channel_id=1, source_target_pairs={{2,0},{4,2},{6,4},{8,6},{10,8},{12,10},{14,12},{16,14},{18,16},{20... | collective-permute-start | bytes 589832 | tf_op jit(solution)/shard_map/ppermute | solution.py:26
  32.0 3.9 copy-start.6
  35.8 2.7 copy-start.11
  35.8 6.0 %copy-start.12 = (f32[80]{0:T(128)S(1)}, f32[80]{0:T(128)}, u32[]{:S(2)}) copy-start(f32[80]{0:T(128)} %param.18) | copy-start | bytes 964
  35.8 6.0 %copy-start.9 = (s32[80]{0:T(128)S(1)}, s32[80]{0:T(128)}, u32[]{:S(2)}) copy-start(s32[80]{0:T(128)} %param.20) | copy-start | bytes 964
  35.9 6.0 %copy-start.10 = (f32[80]{0:T(128)S(1)}, f32[80]{0:T(128)}, u32[]{:S(2)}) copy-start(f32[80]{0:T(128)} %param.17) | copy-start | bytes 964
  35.9 9.8 %copy-start.7 = (s32[32,8]{0,1:T(8,128)S(1)}, s32[32,8]{0,1:T(8,128)}, u32[]{:S(2)}) copy-start(s32[32,8]{0,1:T(8,128)} %param.15) | copy-start | bytes 3076
  51.8 5.7 %copy-start.13 = (s32[128]{0:T(128)S(1)}, s32[128]{0:T(128)}, u32[]{:S(2)}) copy-start(s32[128]{0:T(128)} %param.21) | copy-start | bytes 1540
  103.7 48.0 %collective-permute-start.2 = (f32[3,18,1,256]{3,2,1,0:T(1,128)}, f32[3,18,1,256]{3,2,1,0:T(1,128)S(1)}, u32[]{:S(2)}, u32[]{:S(2)}) collective-permute-start(f32[3,18,1,256]{3,2,1,0:T(1,128)} %get-tuple-element.6), channel_id=1, source_target_pairs={{1,0},{0,1},{3,2},{2,3},{5,4},{4,5},{7,6},{6,7},{9,8},{8,9},{11,10... | collective-permute-start | bytes 165896 | tf_op jit(solution)/shard_map/ppermute | solution.py:26
  106.8 44.9 %collective-permute-start.3 = (f32[3,18,1,256]{3,2,1,0:T(1,128)}, f32[3,18,1,256]{3,2,1,0:T(1,128)}, u32[]{:S(2)}, u32[]{:S(2)}) collective-permute-start(f32[3,18,1,256]{3,2,1,0:T(1,128)} %get-tuple-element.7), channel_id=1, source_target_pairs={{0,1},{1,0},{2,3},{3,2},{4,5},{5,4},{6,7},{7,6},{8,9},{9,8},{10,11... | collective-permute-start | bytes 165896 | tf_op jit(solution)/shard_map/ppermute | solution.py:23
  106.8 63.7 %all-to-all-start.1 = ((bf16[128,2,3,2048]{3,1,2,0:T(2,128)(2,1)}), bf16[128,2,3,2048]{3,1,2,0:T(2,128)(2,1)}, u32[]{:S(2)}, u32[]{:S(2)}) async-start(bf16[128,2,3,2048]{3,1,2,0:T(2,128)(2,1)} %copy.136), calls=%async_computation.1 | async-start | bytes 6291456 | tf_op jit(solution)/shard_map/all_to_all | solution.py:176
  122.8 5.7 %copy-start.8 = (s32[128]{0:T(128)S(1)}, s32[128]{0:T(128)}, u32[]{:S(2)}) copy-start(s32[128]{0:T(128)} %param.14) | copy-start | bytes 1540
  146.0 2.8 copy-start.4
  147.6 2.6 copy-start.5
  193.4 1.4 copy-start.2
  201.0 1.7 copy-start.3
  371.8 40.1 %collective-permute-start.4 = (f32[3,1,64,256]{3,2,1,0:T(8,128)}, f32[3,1,64,256]{3,2,1,0:T(8,128)}, u32[]{:S(2)}, u32[]{:S(2)}) collective-permute-start(f32[3,1,64,256]{3,2,1,0:T(8,128)} %get-tuple-element.19), channel_id=1, source_target_pairs={{2,0},{4,2},{6,4},{8,6},{10,8},{12,10},{14,12},{16,14},{18,16},{20... | collective-permute-start | bytes 589832 | tf_op jit(solution)/shard_map/ppermute | solution.py:26
  378.6 33.4 %collective-permute-start.5 = (f32[3,1,64,256]{3,2,1,0:T(8,128)}, f32[3,1,64,256]{3,2,1,0:T(8,128)}, u32[]{:S(2)}, u32[]{:S(2)}) collective-permute-start(f32[3,1,64,256]{3,2,1,0:T(8,128)} %get-tuple-element.18), channel_id=1, source_target_pairs={{0,2},{2,4},{4,6},{6,8},{8,10},{10,12},{12,14},{14,16},{16,18},{18... | collective-permute-start | bytes 589832 | tf_op jit(solution)/shard_map/ppermute | solution.py:23
  413.5 23.7 %collective-permute-start.6 = (f32[3,18,1,256]{3,2,1,0:T(1,128)}, f32[3,18,1,256]{3,2,1,0:T(1,128)}, u32[]{:S(2)}, u32[]{:S(2)}) collective-permute-start(f32[3,18,1,256]{3,2,1,0:T(1,128)} %get-tuple-element.5), channel_id=1, source_target_pairs={{1,0},{0,1},{3,2},{2,3},{5,4},{4,5},{7,6},{6,7},{9,8},{8,9},{11,10... | collective-permute-start | bytes 165896 | tf_op jit(solution)/shard_map/ppermute | solution.py:26
  414.0 23.2 %collective-permute-start.7 = (f32[3,18,1,256]{3,2,1,0:T(1,128)}, f32[3,18,1,256]{3,2,1,0:T(1,128)}, u32[]{:S(2)}, u32[]{:S(2)}) collective-permute-start(f32[3,18,1,256]{3,2,1,0:T(1,128)} %get-tuple-element.4), channel_id=1, source_target_pairs={{0,1},{1,0},{2,3},{3,2},{4,5},{5,4},{6,7},{7,6},{8,9},{9,8},{10,11... | collective-permute-start | bytes 165896 | tf_op jit(solution)/shard_map/ppermute | solution.py:23
